TPU v7x, 32 devices: a whole 2x2x4 slice. The times are simulated.
32 devices in a mesh: users: 8 (over z, x), items: 4 (over y, core).
Axes of the slice: x: 2, y: 2, z: 4, core: 2. Of those that a mesh axis runs over, the one named last changes fastest.
Arguments:
- tile_users: int32 [8, 4, 128], P('users', 'items'), may hold values from 0 to 127
- tile_owners: int32 [8, 4, 128, 1], P('users', 'items'), may hold values from 0 to 7; in each aligned block of 128 rows (0 to 127, 128 to 255, ..., all dimensions but the last counted through in order) at most 32 rows name the same one
- tile_blocks: int32 [8, 4, 128], P('users', 'items'), may hold values from 0 to 63
- tile_contexts: int32 [8, 4, 128], P('users', 'items'), may hold values from 0 to 7
- row_users: int32 [8, 4, 128, 128], P('users', 'items'), may hold values from 0 to 15
- row_items: int32 [8, 4, 128, 128], P('users', 'items'), may hold values from 0 to 15
- row_contexts: int32 [8, 4, 128, 128], P('users', 'items'), may hold values from 0 to 127
- tile_values: bfloat16 [8, 4, 128, 128], P('users', 'items'), may hold values from -49152 to 49152
- tile_count: int32 [8, 4], P('users', 'items'), may hold values from 64 to 128, as said below
- item_factors: bfloat16 [8192, 256], P('users'), may hold values from -0.125 to 0.25
- context_factors: bfloat16 [1024, 256], replicated, may hold values from -0.125 to 0.25
- profile: bfloat16 [16384, 2048], P('users', 'items'), may hold values from -192 to 192
- feature_factors: bfloat16 [2048, 256], P('items'), may hold values from -6 to 6
Outputs:
- user_factors: bfloat16 [16384, 256], P('users')
- feature_new: bfloat16 [2048, 256], P('items')
Inputs may be any that keep to these rules, and one draw needn't show every extreme that they name: On one device at most 32 tiles name one index of users in tile_owners, a bound that some block reaches. The live tiles of a device are its first tile_count tiles; some device has all 128 live.
All inputs are finite; a program needn't handle non-finite values.
Results may differ from a plain program's by a relative error of at most 0.00155.
The roundings to bfloat16 on the way count: a program that leaves them out, or rounds other values in their place, can miss the bound.
Values may be sent and summed in bfloat16 or wider, within the bound.
No kernel may reach another device: no remote copies, remote signals or barrier semaphores. Data moves between devices by JAX's collectives and lax.ppermute only.
A program may use at most 64 MiB of HBM per device.

v0:
```python
import jax
import jax.numpy as jnp
from jax import lax
from jax.sharding import PartitionSpec as P

CB = 128
IB = 16
UB = 16
RIDGE = 1.0


def gram(matrix):
    return lax.dot_general(
        matrix, matrix, (((0,), (0,)), ((), ())), preferred_element_type=jnp.float32
    )


def solve_rows(normal, right_side):
    cholesky_factor = jnp.linalg.cholesky(normal)
    return jax.scipy.linalg.cho_solve((cholesky_factor, True), right_side.T).T


def local(
    tile_users,
    tile_owners,
    tile_blocks,
    tile_contexts,
    row_users,
    row_items,
    row_contexts,
    tile_values,
    tile_count,
    item_factors,
    context_factors,
    profile,
    feature_factors,
):
    users_size = lax.axis_size("users")
    tile_total = tile_users.shape[2]
    rank_width = item_factors.shape[1]
    slab_users = profile.shape[0]
    blocks_held = item_factors.shape[0] // IB
    capacity = max(2, 2 * tile_total // users_size)
    owners = tile_owners.reshape(tile_total)
    local_block = tile_blocks.reshape(tile_total)
    live_count = tile_count.reshape(())
    position = jnp.arange(tile_total, dtype=jnp.int32)
    same_owner = (owners[:, None] == owners[None, :]) & (position[None, :] < position[:, None])
    slot_rank = jnp.sum(same_owner.astype(jnp.int32), axis=1)
    tile_place = owners * capacity + slot_rank
    request_block = jnp.where(position < live_count, local_block, 0)
    wanted = jnp.zeros((users_size * capacity,), jnp.int32).at[tile_place].set(request_block)
    asked_blocks = lax.all_to_all(
        wanted.reshape(users_size, capacity), "users", split_axis=0, concat_axis=0, tiled=True
    )
    shard_blocks = item_factors.reshape(blocks_held, IB, rank_width)
    answered = shard_blocks[asked_blocks.reshape(-1)].reshape(users_size, capacity, IB, rank_width)
    fetched = lax.all_to_all(answered, "users", split_axis=0, concat_axis=0, tiled=True).reshape(
        users_size * capacity, IB, rank_width
    )
    identity = jnp.eye(rank_width, dtype=jnp.float32)
    context_gram = gram(context_factors)
    item_gram = lax.psum(gram(item_factors), "users")
    feature_gram = lax.psum(gram(feature_factors), "items")
    normal = item_gram * context_gram + feature_gram
    normal = normal + RIDGE * identity
    user_blocks = slab_users // UB
    context_table = context_factors.reshape(-1, CB, rank_width)
    tile_ublock = tile_users.reshape(tile_total)
    tile_cblock = tile_contexts.reshape(tile_total)
    users_rows = row_users.reshape(tile_total, -1)
    items_rows = row_items.reshape(tile_total, -1)
    contexts_rows = row_contexts.reshape(tile_total, -1)
    values_rows = tile_values.reshape(tile_total, -1)
    group_size = 16

    def add_group(step_index, running):
        first_tile = step_index * group_size

        def window(source):
            return lax.dynamic_slice_in_dim(source, first_tile, group_size, 0)

        item_blocks = fetched[window(tile_place)]
        context_blocks = context_table[window(tile_cblock)]
        item_onehot = (
            window(items_rows)[:, :, None] == jnp.arange(IB, dtype=jnp.int32)[None, None, :]
        ).astype(jnp.bfloat16)
        context_onehot = (
            window(contexts_rows)[:, :, None] == jnp.arange(CB, dtype=jnp.int32)[None, None, :]
        ).astype(jnp.bfloat16)
        item_rows_sel = jnp.einsum(
            "gti,gir->gtr", item_onehot, item_blocks, preferred_element_type=jnp.float32
        )
        context_rows_sel = jnp.einsum(
            "gtc,gcr->gtr", context_onehot, context_blocks, preferred_element_type=jnp.float32
        )
        alive_mask = (first_tile + jnp.arange(group_size, dtype=jnp.int32) < live_count).astype(
            jnp.float32
        )
        weighted = window(values_rows).astype(jnp.float32) * alive_mask[:, None]
        row_terms = weighted[:, :, None] * item_rows_sel * context_rows_sel
        user_onehot = (
            window(users_rows)[:, None, :] == jnp.arange(UB, dtype=jnp.int32)[None, :, None]
        ).astype(jnp.float32)
        per_tile = jnp.einsum(
            "gut,gtr->gur", user_onehot, row_terms, precision=lax.Precision.HIGHEST
        )
        block_onehot = (
            window(tile_ublock)[None, :] == jnp.arange(user_blocks, dtype=jnp.int32)[:, None]
        ).astype(jnp.float32)
        return running + jnp.einsum(
            "bg,gur->bur", block_onehot, per_tile, precision=lax.Precision.HIGHEST
        )

    rounds = (live_count + group_size - 1) // group_size
    mttkrp = lax.fori_loop(
        0, rounds, add_group, jnp.zeros((user_blocks, UB, rank_width), jnp.float32)
    ).reshape(slab_users, rank_width)
    local_right = mttkrp + jnp.dot(profile, feature_factors, preferred_element_type=jnp.float32)
    right_side = lax.psum(local_right, "items")
    user_factors = solve_rows(normal, right_side).astype(jnp.bfloat16)
    feature_terms = lax.dot_general(
        profile, user_factors, (((0,), (0,)), ((), ())), preferred_element_type=jnp.float32
    )
    user_gram, feature_right = lax.psum((gram(user_factors), feature_terms), "users")
    feature_new = solve_rows(user_gram + RIDGE * identity, feature_right).astype(jnp.bfloat16)
    return (user_factors, feature_new)


def solution(mesh):
    in_specs = (
        P("users", "items", None),
        P("users", "items", None, None),
        P("users", "items", None),
        P("users", "items", None),
        P("users", "items", None, None),
        P("users", "items", None, None),
        P("users", "items", None, None),
        P("users", "items", None, None),
        P("users", "items"),
        P("users", None),
        P(),
        P("users", "items"),
        P("items", None),
    )
    out_specs = (P("users", None), P("items", None))
    return jax.shard_map(local, mesh=mesh, in_specs=in_specs, out_specs=out_specs, check_vma=False)
```

profile of v0, /device:TPU:0, one launch (start us, length us, event | category | flops | bytes accessed | tf_op | source)
XLA Modules:
  0.0 481.4 jit_solution(13912460111386983107)
XLA Ops:
  11.3 13.6 %all_to_all.14 = s32[8,1,32]{2,1,0:T(1,128)S(1)} all-to-all(s32[8,1,32]{2,1,0:T(1,128)S(1)} %all_to_all.9), channel_id=1, replica_groups=mesh['users'=8,'items'=4] {'users'}, dimensions={0} | all-to-all | bytes 2048 | tf_op jit(solution)/shard_map/all_to_all | solution.py:53
  29.2 4.5 all-to-all-start.1
  35.9 48.9 %all-to-all-done.1 = bf16[8,32,16,256]{3,2,1,0:T(8,128)(2,1)} async-done(((bf16[8,32,16,256]{3,2,1,0:T(8,128)(2,1)}), bf16[8,32,16,256]{3,2,1,0:T(8,128)(2,1)}, u32[]{:S(2)}, u32[]{:S(2)}) %all-to-all-start.1) | async-done | bytes 2097184 | tf_op jit(solution)/shard_map/all_to_all | solution.py:58
  86.4 115.0 %while.12 = (s32[]{:T(128)}, f32[128,16,256]{2,0,1:T(8,128)}, s32[]{:T(128)}, s32[128]{0:T(128)S(1)}, s32[128,128]{1,0:T(8,128)}, /*index=5*/bf16[128,128]{1,0:T...) while((s32[]{:T(128)}, f32[128,16,256]{2,0,1:T(8,128)}, ...), condition=%wide.region_9.11_spmd, body=%wide.region_8.10_spmd.sunk | while | flops 354230400 | bytes 25138244 | solution.py:116
  96.7 4.0 convolution_add_fusion.3
  111.1 4.0 convolution_add_fusion.3
  125.5 4.0 convolution_add_fusion.3
  139.9 4.0 convolution_add_fusion.3
  154.3 4.0 convolution_add_fusion.3
  168.6 4.0 convolution_add_fusion.3
  183.0 4.0 convolution_add_fusion.3
  197.4 4.0 convolution_add_fusion.3
  206.9 54.0 %all-reduce.11.cloned.1.call-done = (f32[256,2048]{0,1:T(8,128)}, f32[256,256]{0,1:T(8,128)}) async-done(((f32[256,2048]{0,1:T(8,128)}, f32[256,256]{0,1:T(8,128)}), (f32[256,2048]{0,1:T(8,128)}, f32[256,256]{0,1:T(8,128)})) %all-reduce.11.cloned.1.call-update) | async-done | bytes 2359312 | tf_op jit(solution)/shard_map/psum | solution.py:120
  262.5 11.7 %cholesky.130 = f32[128,128]{1,0:T(8,128)S(1)} custom-call(f32[128,128]{1,0:T(8,128)S(1)} %cholesky.194), custom_call_target="Cholesky" | custom-call | tf_op jit(solution)/shard_map/jit(cholesky)/cholesky | solution.py:19
  274.3 9.8 %custom-call.25 = f32[1,128,128]{1,2,0:T(8,128)S(1)} custom-call(f32[1,128,128]{2,1,0:T(8,128)S(1)} %get-tuple-element.153), custom_call_target="InvertDiagBlocksLowerTriangular" | custom-call | tf_op jit(solution)/shard_map/jit(cholesky)/cholesky | solution.py:19
  284.6 11.7 %cholesky.147 = f32[128,128]{1,0:T(8,128)S(1)} custom-call(f32[128,128]{1,0:T(8,128)S(1)} %convolution_subtract_fusion.5), custom_call_target="Cholesky" | custom-call | tf_op jit(solution)/shard_map/jit(cholesky)/cholesky | solution.py:19
  298.4 4.2 while.13
  302.6 19.7 %custom-call.22 = f32[2,128,128]{1,2,0:T(8,128)S(1)} custom-call(f32[2,128,128]{2,1,0:T(8,128)S(1)} %get-tuple-element.79), custom_call_target="InvertDiagBlocksLowerTriangular" | custom-call | tf_op jit(solution)/shard_map/jit(_cho_solve)/triangular_solve | solution.py:20
  336.2 72.6 %all-reduce.9.cloned.1.call-done = (f32[256,512]{1,0:T(8,128)}, f32[256,256]{0,1:T(8,128)}) async-done(((f32[256,512]{1,0:T(8,128)}, f32[256,256]{0,1:T(8,128)}), (f32[256,512]{1,0:T(8,128)}, f32[256,256]{0,1:T(8,128)})) %all-reduce.9.cloned.1.call-update) | async-done | bytes 786448 | tf_op jit(solution)/shard_map/psum | solution.py:125
  411.0 11.7 %cholesky.164 = f32[128,128]{1,0:T(8,128)S(1)} custom-call(f32[128,128]{1,0:T(8,128)S(1)} %cholesky.197), custom_call_target="Cholesky" | custom-call | tf_op jit(solution)/shard_map/jit(cholesky)/cholesky | solution.py:19
  422.8 9.8 %custom-call.26 = f32[1,128,128]{1,2,0:T(8,128)S(1)} custom-call(f32[1,128,128]{2,1,0:T(8,128)S(1)} %get-tuple-element.149), custom_call_target="InvertDiagBlocksLowerTriangular" | custom-call | tf_op jit(solution)/shard_map/jit(cholesky)/cholesky | solution.py:19
  433.1 11.7 %cholesky.181 = f32[128,128]{1,0:T(8,128)S(1)} custom-call(f32[128,128]{1,0:T(8,128)S(1)} %convolution_subtract_fusion.4), custom_call_target="Cholesky" | custom-call | tf_op jit(solution)/shard_map/jit(cholesky)/cholesky | solution.py:19
  447.5 3.9 while.14
  451.4 19.9 %custom-call.23 = f32[2,128,128]{1,2,0:T(8,128)S(1)} custom-call(f32[2,128,128]{2,1,0:T(8,128)S(1)} %get-tuple-element.87), custom_call_target="InvertDiagBlocksLowerTriangular" | custom-call | tf_op jit(solution)/shard_map/jit(_cho_solve)/triangular_solve | solution.py:20
  (223 shorter events, 131.3 us)
Async XLA Ops:
  7.2 197.0 %copy-start = (bf16[2048,512]{1,0:T(8,128)(2,1)S(1)}, bf16[2048,512]{1,0:T(8,128)(2,1)}, u32[]{:S(2)}) copy-start(bf16[2048,512]{1,0:T(8,128)(2,1)} %param.27) | copy-start | bytes 6291460
  29.2 4.6 copy-start.3
  29.2 5.7 %copy-start.10 = (s32[1,1,128,1]{2,3,1,0:T(1,128)S(1)}, s32[1,1,128,1]{2,3,1,0:T(1,128)}, u32[]{:S(2)}) copy-start(s32[1,1,128,1]{2,3,1,0:T(1,128)} %param.17) | copy-start | bytes 1540
  29.2 5.7 %copy-start.4 = (bf16[512,256]{1,0:T(8,128)(2,1)S(1)}, bf16[512,256]{1,0:T(8,128)(2,1)}, u32[]{:S(2)}) copy-start(bf16[512,256]{1,0:T(8,128)(2,1)} %param.28) | copy-start | bytes 786436
  29.2 55.6 %all-to-all-start.1 = ((bf16[8,32,16,256]{3,2,1,0:T(8,128)(2,1)}), bf16[8,32,16,256]{3,2,1,0:T(8,128)(2,1)}, u32[]{:S(2)}, u32[]{:S(2)}) async-start(bf16[8,32,16,256]{3,2,1,0:T(8,128)(2,1)} %bitcast.133), calls=%async_computation.1 | async-start | bytes 4194304 | tf_op jit(solution)/shard_map/all_to_all | solution.py:58
  33.7 52.7 %copy-start.9 = (s32[1,1,128]{2,1,0:T(1,128)S(1)}, s32[1,1,128]{2,1,0:T(1,128)}, u32[]{:S(2)}) copy-start(s32[1,1,128]{2,1,0:T(1,128)} %param.19) | copy-start | bytes 1540
  33.7 52.7 %copy-start.11 = (s32[1,1,128]{2,1,0:T(1,128)S(1)}, s32[1,1,128]{2,1,0:T(1,128)}, u32[]{:S(2)}) copy-start(s32[1,1,128]{2,1,0:T(1,128)} %param.16) | copy-start | bytes 1540
  33.7 173.2 %all-reduce.7.cloned.1.call-start = ((), (), s32[]{:S(2)}) async-start(), calls=%async_computation.2 | async-start | bytes 524288 | tf_op jit(solution)/shard_map/psum | solution.py:63
  34.8 226.1 %all-reduce.11.cloned.1.call-start = ((), (), s32[]{:S(2)}) async-start(), calls=%async_computation.4 | async-start | bytes 4718592 | tf_op jit(solution)/shard_map/psum | solution.py:120
  92.8 2.9 copy-start.1
  107.2 2.9 copy-start.1
  121.6 2.9 copy-start.1
  136.0 2.9 copy-start.1
  150.3 2.9 copy-start.1
  164.7 2.9 copy-start.1
  179.1 2.9 copy-start.1
  193.4 2.9 copy-start.1
  206.2 54.7 %copy-start.2 = (bf16[8,128,256]{2,1,0:T(8,128)(2,1)S(1)}, bf16[8,128,256]{2,1,0:T(8,128)(2,1)}, u32[]{:S(2)}) copy-start(bf16[8,128,256]{2,1,0:T(8,128)(2,1)} %get-tuple-element.400) | copy-start | bytes 1572868
  206.3 202.6 %all-reduce.9.cloned.1.call-start = ((), (), s32[]{:S(2)}) async-start(), calls=%async_computation.3 | async-start | bytes 1572864 | tf_op jit(solution)/shard_map/psum | solution.py:125
  322.2 2.5 copy-start.5
  328.6 3.3 copy-start.7
  330.7 1.2 copy-start.6
  409.8 61.5 %copy-start.8 = (f32[256,512]{1,0:T(8,128)S(1)}, f32[256,512]{1,0:T(8,128)}, u32[]{:S(2)}) copy-start(f32[256,512]{1,0:T(8,128)} %get-tuple-element.134) | copy-start | bytes 1572868
Sparse Core Ops, SparseCore 0:
  38.5 86.4 all-reduce.6
  206.4 54.4 all-reduce.10
  333.6 75.2 all-reduce.8
where the time goes:
time: 489 us; the launch traced here: 481 us
  waiting for transfers between devices  176 us (36%)
  other arithmetic  126 us (26%)
  matrix products  80.1 us (16%)
  local copies, waits for them, and re-layouts  62.1 us (13%)
  between operations  17.8 us (4%)
  blocking collectives  13.6 us (3%)
  starting transfers between devices  5.11 us (1%)
    psum x1, waiting for transfers between devices, local(): lax.psum((gram(user_factors), feature_terms), 'users')  72.6 us
    another operation x13, other arithmetic, solve_rows(): cholesky_factor = jnp.linalg.cholesky(normal)  68.6 us
    psum x1, waiting for transfers between devices, local(): right_side = lax.psum(local_right, 'items')  54 us
    all_to_all x1, waiting for transfers between devices, local(): lax.all_to_all(answered, 'users', split_axis=0, concat_axis=0, tiled=True)  48.9 us
    another operation x5, other arithmetic, solve_rows(): return jax.scipy.linalg.cho_solve((cholesky_factor, True), right_side.T).T  39.7 us
    dot_general x8, matrix products, add_group(): jnp.einsum('bg,gur->bur', block_onehot, per_tile, precision=lax.Precision...  32 us
    gather x8, local copies, waits for them, and re-layouts, add_group(): item_blocks = fetched[window(tile_place)]  17.2 us
    dot_general x8, matrix products, add_group(): jnp.einsum('gtc,gcr->gtr', context_onehot, context_blocks, preferred_elem...  14.5 us
  transfers between devices with their start and end apart: 4, of which 3 were waited for; matrix products, arithmetic and copies ran while one was open for 26% of the time, Pallas kernels for 0%

commit v1 on v0

--- a/solution.py
+++ b/solution.py
@@ -7,6 +7,12 @@
 IB = 16
 UB = 16
 RIDGE = 1.0
+
+
+def add_all(value, mesh_axis):
+    parts = lax.all_gather(value, mesh_axis, axis=0, tiled=False)
+    total = parts.sum(axis=0)
+    return total
 
 
 def gram(matrix):
@@ -117,7 +123,7 @@
         0, rounds, add_group, jnp.zeros((user_blocks, UB, rank_width), jnp.float32)
     ).reshape(slab_users, rank_width)
     local_right = mttkrp + jnp.dot(profile, feature_factors, preferred_element_type=jnp.float32)
-    right_side = lax.psum(local_right, "items")
+    right_side = add_all(local_right, "items")
     user_factors = solve_rows(normal, right_side).astype(jnp.bfloat16)
     feature_terms = lax.dot_general(
         profile, user_factors, (((0,), (0,)), ((), ())), preferred_element_type=jnp.float32

time: 489 us -> 436 us (0.89)
  waiting for transfers between devices: 176 us -> 117 us
  other arithmetic: 126 us -> 132 us
    psum x1, waiting for transfers between devices: 54 us -> 0.02 us  [local(): feature_gram = lax.psum(gram(feature_factors), 'items')]
    reduce_sum x0 -> x1, other arithmetic: none -> 5.6 us  [add_all(): total = parts.sum(axis=0)]
  transfers between devices with their start and end apart: 4 -> 5, of which waited for: 3 -> 2; matrix products, arithmetic and copies ran while one was open for 26% -> 43% of each run, Pallas kernels for 0% -> 0%
where the time goes in v1:
time: 436 us; the launch traced here: 428 us
  other arithmetic  132 us (30%)
  waiting for transfers between devices  117 us (27%)
  matrix products  80.2 us (18%)
  local copies, waits for them, and re-layouts  62.4 us (14%)
  between operations  17.8 us (4%)
  blocking collectives  13.6 us (3%)
  starting transfers between devices  5.16 us (1%)
    psum x1, waiting for transfers between devices, local(): lax.psum((gram(user_factors), feature_terms), 'users')  71.7 us
    another operation x13, other arithmetic, solve_rows(): cholesky_factor = jnp.linalg.cholesky(normal)  68.5 us
    all_to_all x1, waiting for transfers between devices, local(): lax.all_to_all(answered, 'users', split_axis=0, concat_axis=0, tiled=True)  44.8 us
    another operation x5, other arithmetic, solve_rows(): return jax.scipy.linalg.cho_solve((cholesky_factor, True), right_side.T).T  39.7 us
    dot_general x8, matrix products, add_group(): jnp.einsum('bg,gur->bur', block_onehot, per_tile, precision=lax.Precision...  32 us
    gather x8, local copies, waits for them, and re-layouts, add_group(): item_blocks = fetched[window(tile_place)]  17.2 us
    dot_general x8, matrix products, add_group(): jnp.einsum('gtc,gcr->gtr', context_onehot, context_blocks, preferred_elem...  14.5 us
    all_to_all x1, blocking collectives, local(): lax.all_to_all(wanted.reshape(users_size, capacity), 'users', split_axis=...  13.6 us
  transfers between devices with their start and end apart: 5, of which 2 were waited for; matrix products, arithmetic and copies ran while one was open for 43% of the time, Pallas kernels for 0%

profile of v1, /device:TPU:0, one launch (start us, length us, event | category | flops | bytes accessed | tf_op | source)
XLA Modules:
  0.0 428.5 jit_solution(12400405044412644359)
XLA Ops:
  11.3 13.6 %all_to_all.14 = s32[8,1,32]{2,1,0:T(1,128)S(1)} all-to-all(s32[8,1,32]{2,1,0:T(1,128)S(1)} %all_to_all.9), channel_id=1, replica_groups=mesh['users'=8,'items'=4] {'users'}, dimensions={0} | all-to-all | bytes 2048 | tf_op jit(solution)/shard_map/all_to_all | solution.py:59
  29.2 4.5 %all-to-all-start.1 = ((bf16[8,32,16,256]{3,2,1,0:T(8,128)(2,1)}), bf16[8,32,16,256]{3,2,1,0:T(8,128)(2,1)}, u32[]{:S(2)}, u32[]{:S(2)}) async-start(bf16[8,32,16,256]{3,2,1,0:T(8,128)(2,1)} %bitcast.133), calls=%async_computation.1 | async-start | bytes 4194304 | tf_op jit(solution)/shard_map/all_to_all | solution.py:64
  36.0 44.8 %all-to-all-done.1 = bf16[8,32,16,256]{3,2,1,0:T(8,128)(2,1)} async-done(((bf16[8,32,16,256]{3,2,1,0:T(8,128)(2,1)}), bf16[8,32,16,256]{3,2,1,0:T(8,128)(2,1)}, u32[]{:S(2)}, u32[]{:S(2)}) %all-to-all-start.1) | async-done | bytes 2097184 | tf_op jit(solution)/shard_map/all_to_all | solution.py:64
  82.3 115.1 %while.12 = (s32[]{:T(128)}, f32[128,16,256]{2,0,1:T(8,128)}, s32[]{:T(128)}, s32[128]{0:T(128)S(1)}, s32[128,128]{1,0:T(8,128)}, /*index=5*/bf16[128,128]{1,0:T...) while((s32[]{:T(128)}, f32[128,16,256]{2,0,1:T(8,128)}, ...), condition=%wide.region_9.11_spmd, body=%wide.region_8.10_spmd.sunk | while | flops 354230400 | bytes 25138244 | solution.py:122
  92.7 4.0 convolution_add_fusion.3
  107.1 4.0 convolution_add_fusion.3
  121.5 4.0 convolution_add_fusion.3
  135.9 4.0 convolution_add_fusion.3
  150.3 4.0 convolution_add_fusion.3
  164.6 4.0 convolution_add_fusion.3
  179.0 4.0 convolution_add_fusion.3
  193.4 4.0 convolution_add_fusion.3
  204.9 11.7 %cholesky.130 = f32[128,128]{1,0:T(8,128)S(1)} custom-call(f32[128,128]{1,0:T(8,128)S(1)} %cholesky.194), custom_call_target="Cholesky" | custom-call | tf_op jit(solution)/shard_map/jit(cholesky)/cholesky | solution.py:25
  216.7 9.8 %custom-call.25 = f32[1,128,128]{1,2,0:T(8,128)S(1)} custom-call(f32[1,128,128]{2,1,0:T(8,128)S(1)} %get-tuple-element.151), custom_call_target="InvertDiagBlocksLowerTriangular" | custom-call | tf_op jit(solution)/shard_map/jit(cholesky)/cholesky | solution.py:25
  227.0 11.7 %cholesky.147 = f32[128,128]{1,0:T(8,128)S(1)} custom-call(f32[128,128]{1,0:T(8,128)S(1)} %convolution_subtract_fusion.5), custom_call_target="Cholesky" | custom-call | tf_op jit(solution)/shard_map/jit(cholesky)/cholesky | solution.py:25
  240.8 4.2 while.13
  245.0 19.7 %custom-call.22 = f32[2,128,128]{1,2,0:T(8,128)S(1)} custom-call(f32[2,128,128]{2,1,0:T(8,128)S(1)} %get-tuple-element.79), custom_call_target="InvertDiagBlocksLowerTriangular" | custom-call | tf_op jit(solution)/shard_map/jit(_cho_solve)/triangular_solve | solution.py:26
  264.7 5.6 %reduce_sum.22 = f32[2048,256]{1,0:T(8,128)} reduce(f32[4,2048,256]{2,1,0:T(8,128)} %bitcast.134, f32[]{:T(128)} %constant.121.clone.1), dimensions={0}, to_apply=%region_10.12 | reduce | flops 1572864 | bytes 10485764 | tf_op jit(solution)/shard_map/reduce_sum | solution.py:14
  284.4 71.7 %all-reduce.10.cloned.1.call-done = (f32[256,512]{1,0:T(8,128)}, f32[256,256]{0,1:T(8,128)}) async-done(((f32[256,512]{1,0:T(8,128)}, f32[256,256]{0,1:T(8,128)}), (f32[256,512]{1,0:T(8,128)}, f32[256,256]{0,1:T(8,128)})) %all-reduce.10.cloned.1.call-update) | async-done | bytes 786448 | tf_op jit(solution)/shard_map/psum | solution.py:131
  358.2 11.7 %cholesky.164 = f32[128,128]{1,0:T(8,128)S(1)} custom-call(f32[128,128]{1,0:T(8,128)S(1)} %cholesky.197), custom_call_target="Cholesky" | custom-call | tf_op jit(solution)/shard_map/jit(cholesky)/cholesky | solution.py:25
  370.0 9.8 %custom-call.26 = f32[1,128,128]{1,2,0:T(8,128)S(1)} custom-call(f32[1,128,128]{2,1,0:T(8,128)S(1)} %get-tuple-element.147), custom_call_target="InvertDiagBlocksLowerTriangular" | custom-call | tf_op jit(solution)/shard_map/jit(cholesky)/cholesky | solution.py:25
  380.3 11.7 %cholesky.181 = f32[128,128]{1,0:T(8,128)S(1)} custom-call(f32[128,128]{1,0:T(8,128)S(1)} %convolution_subtract_fusion.4), custom_call_target="Cholesky" | custom-call | tf_op jit(solution)/shard_map/jit(cholesky)/cholesky | solution.py:25
  394.6 3.8 while.14
  398.4 19.9 %custom-call.23 = f32[2,128,128]{1,2,0:T(8,128)S(1)} custom-call(f32[2,128,128]{2,1,0:T(8,128)S(1)} %get-tuple-element.87), custom_call_target="InvertDiagBlocksLowerTriangular" | custom-call | tf_op jit(solution)/shard_map/jit(_cho_solve)/triangular_solve | solution.py:26
  (227 shorter events, 131.9 us)
Async XLA Ops:
  7.2 193.0 %copy-start = (bf16[2048,512]{1,0:T(8,128)(2,1)S(1)}, bf16[2048,512]{1,0:T(8,128)(2,1)}, u32[]{:S(2)}) copy-start(bf16[2048,512]{1,0:T(8,128)(2,1)} %param.27) | copy-start | bytes 6291460
  29.2 4.5 %copy-start.5 = (bf16[512,256]{1,0:T(8,128)(2,1)S(1)}, bf16[512,256]{1,0:T(8,128)(2,1)}, u32[]{:S(2)}) copy-start(bf16[512,256]{1,0:T(8,128)(2,1)} %param.28) | copy-start | bytes 786436
  29.2 5.6 %copy-start.3 = (bf16[1024,256]{1,0:T(8,128)(2,1)S(1)}, bf16[1024,256]{1,0:T(8,128)(2,1)}, u32[]{:S(2)}) copy-start(bf16[1024,256]{1,0:T(8,128)(2,1)} %param.25) | copy-start | bytes 1572868
  29.2 51.6 %all-to-all-start.1 = ((bf16[8,32,16,256]{3,2,1,0:T(8,128)(2,1)}), bf16[8,32,16,256]{3,2,1,0:T(8,128)(2,1)}, u32[]{:S(2)}, u32[]{:S(2)}) async-start(bf16[8,32,16,256]{3,2,1,0:T(8,128)(2,1)} %bitcast.133), calls=%async_computation.1 | async-start | bytes 4194304 | tf_op jit(solution)/shard_map/all_to_all | solution.py:64
  33.7 2.3 copy-start.10
  33.7 169.3 %all-reduce.8.cloned.1.call-start = ((), (), s32[]{:S(2)}) async-start(), calls=%async_computation.3 | async-start | bytes 524288 | tf_op jit(solution)/shard_map/psum | solution.py:70
  34.7 47.6 %copy-start.9 = (s32[1,1,128]{2,1,0:T(1,128)S(1)}, s32[1,1,128]{2,1,0:T(1,128)}, u32[]{:S(2)}) copy-start(s32[1,1,128]{2,1,0:T(1,128)} %param.19) | copy-start | bytes 1540
  34.7 47.6 %copy-start.11 = (s32[1,1,128]{2,1,0:T(1,128)S(1)}, s32[1,1,128]{2,1,0:T(1,128)}, u32[]{:S(2)}) copy-start(s32[1,1,128]{2,1,0:T(1,128)} %param.16) | copy-start | bytes 1540
  34.8 168.2 %all-reduce.6.cloned.1.call-start = ((), (), s32[]{:S(2)}) async-start(), calls=%async_computation.2 | async-start | bytes 524288 | tf_op jit(solution)/shard_map/psum | solution.py:69
  35.9 228.8 %all-gather.3.cloned.1.call-start = ((), (), s32[]{:S(2)}) async-start(), calls=%async_computation.4 | async-start | bytes 10485760 | tf_op jit(solution)/shard_map/all_gather | solution.py:13
  88.8 2.9 copy-start.1
  103.1 2.9 copy-start.1
  117.5 2.9 copy-start.1
  131.9 2.9 copy-start.1
  146.3 2.9 copy-start.1
  160.7 2.9 copy-start.1
  175.1 2.9 copy-start.1
  189.4 2.9 copy-start.1
  202.3 1.0 copy-start.2
  202.4 153.7 %all-reduce.10.cloned.1.call-start = ((), (), s32[]{:S(2)}) async-start(), calls=%async_computation.5 | async-start | bytes 1572864 | tf_op jit(solution)/shard_map/psum | solution.py:131
  270.3 2.4 copy-start.4
  276.7 3.3 copy-start.7
  278.8 1.2 copy-start.6
  357.0 61.3 %copy-start.8 = (f32[256,512]{1,0:T(8,128)S(1)}, f32[256,512]{1,0:T(8,128)}, u32[]{:S(2)}) copy-start(f32[256,512]{1,0:T(8,128)} %get-tuple-element.134) | copy-start | bytes 1572868
Sparse Core Ops, SparseCore 0:
  37.4 33.5 all-reduce.7
  75.0 71.0 all-reduce.5
  202.5 57.4 all-gather.2
  281.7 74.3 all-reduce.9
